TPU v7x, 256 devices: a whole 4x4x8 slice. The times are simulated.
256 devices in a mesh: dp: 4 (over z_hi), expert: 64 (over y, x, z_lo, core).
Axes of the slice: x: 4, y: 4, z: 8 (z_hi: 4, z_lo: 2; z = z_hi * 2 + z_lo), core: 2. Of those that a mesh axis runs over, the one named last changes fastest.
Arguments:
- tokens: bfloat16 [32768, 3584], P(('dp', 'expert')), may hold values from -6 to 6
- cotangent: bfloat16 [32768, 1024], P(('dp', 'expert')), may hold values from -6 to 6
- expert_ids: int32 [32768, 8], P(('dp', 'expert')), may hold values from 0 to 255, all different within a row; in each aligned block of 128 rows (0 to 127, 128 to 255, ...) at most 6 rows name the same one
- gate_values: float32 [32768, 8], P(('dp', 'expert')), may hold values from 0.1 to 1
- counts: int32 [256], P(('dp', 'expert')), may hold values from 64 to 128
- swap_flags: int32 [64], replicated, may hold values from 0 to 1, as said below
- weights: bfloat16 [64, 3584, 1024], P('expert', 'dp'), may hold values from -0.035888672 to 0.035888672
- first_moment: bfloat16 [64, 3584, 1024], P('expert', 'dp'), may hold values from -6 to 6
- second_moment: bfloat16 [64, 3584, 1024], P('expert', 'dp'), may hold values from 1 to 100
Outputs:
- new_weights: bfloat16 [64, 3584, 1024], P('expert', 'dp')
- new_first: bfloat16 [64, 3584, 1024], P('expert', 'dp')
- new_second: bfloat16 [64, 3584, 1024], P('expert', 'dp')
Inputs may be any that keep to these rules, and one draw needn't show every extreme that they name: `expert_ids`: within the 128 rows of one device no expert is named by more than 6 rows; a token names 8 different experts. swap_flags[e] equals swap_flags[(e + 32) mod 64].
All inputs are finite; a program needn't handle non-finite values.
Results may differ from a plain program's by a relative error of at most 0.015.
Values may be sent and summed in bfloat16 or wider, within the bound.
A program may use at most 128 MiB of HBM per device.

v0:
```python
import functools

import jax
import jax.numpy as jnp
from jax import lax
from jax.experimental import pallas as pl
from jax.experimental.pallas import tpu as pltpu
from jax.sharding import PartitionSpec as P

beta_first = 0.9
beta_second = 0.95
bias_first = 1.0 - 0.9**3
bias_second = 1.0 - 0.95**3
learn_rate = 0.005
epsilon = 1e-08
most = 6
f32, bf16, i32 = jnp.float32, jnp.bfloat16, jnp.int32
MESH = pl.DeviceIdType.MESH
near_first = (0, 1, 3, 2)
pieces = 1
PART, PASS, FINISH, FORWARD, MOMENTS = range(5)
order = (
    (PART, 0), (PASS, 0), (PART, 1), (PASS, 1), (PART, 2), (MOMENTS, 0), (MOMENTS, 1), (FINISH, 0), (PASS, 2), (FINISH, 1), (FORWARD, 0), (PART, 3), (FORWARD, 1), (FINISH, 2), (PASS, 3), (FORWARD, 2), (FINISH, 3), (FORWARD, 3),
)


def exchange_kernel(
    nd, ne, planes,
    count, ids, gates, flags, tokens, cot, w, m, v,
    x_out, slopes, w_in, m_in, v_in,
    rx, aux, aux_in, places, weights, send, got, w_own, w_mov, z_send, z_own, z_first, z_right_in, z_left_in, own_slope,
    loc_sem, swap_send, swap_recv, ex_send, ex_recv, a_send, a_recv, f_send, f_recv, d_send, d_recv, r_send, r_recv,
):
    me_d, me_e = lax.axis_index("dp"), lax.axis_index("expert")
    right, left, opp = lax.rem(me_d + 1, nd), lax.rem(me_d + nd - 1, nd), lax.rem(me_d + 2, nd)
    mate = lax.rem(me_e + ne // 2, ne)
    top, tok_rows = ids.shape
    dpart, fpart = tokens.shape[1] // nd, cot.shape[1] // nd
    my_z = lax.rem(me_e // 2, 2)
    pair = me_e + 2 - 4 * my_z
    here = (me_e // 4) * 2 + lax.rem(me_e, 2)
    nh = ne // 2
    sources = 2 * nd
    per_slot = sources * most
    slots_plane = nh // planes
    my_plane = here // slots_plane

    def expert_at(spot):
        return (spot // 2) * 4 + 2 * my_z + lax.rem(spot, 2)

    rows_plane = slots_plane * per_slot
    half = rows_plane // 2

    barrier = pltpu.get_barrier_semaphore()

    def greet(i, carry):
        spot = lax.rem(here + i, nh)
        pl.semaphore_signal(barrier, inc=1, device_id={"expert": expert_at(spot)}, device_id_type=MESH)
        return carry

    lax.fori_loop(1, nh, greet, 0)
    others = [(i, e) for i in range(nd) for e in (me_e, pair)][1:]
    for i, e in others:
        pl.semaphore_signal(barrier, inc=1, device_id={"dp": lax.rem(me_d + i, nd), "expert": e}, device_id_type=MESH)
    pl.semaphore_wait(barrier, nh - 1 + len(others))

    def swap(kind, src, dst):
        return pltpu.make_async_remote_copy(
            src_ref=src, dst_ref=dst, send_sem=swap_send.at[kind], recv_sem=swap_recv.at[kind],
            device_id={"expert": mate}, device_id_type=MESH,
        )

    w_swap = swap(0, w.at[0], w_mov)

    def remote(src, dst, send_sem, recv_sem, dp, expert):
        return pltpu.make_async_remote_copy(
            src_ref=src, dst_ref=dst, send_sem=send_sem, recv_sem=recv_sem,
            device_id={"dp": dp, "expert": expert}, device_id_type=MESH,
        )

    def rows_from(dp, z):
        return pl.ds(pl.multiple_of((z * nd + dp) * tok_rows, tok_rows), tok_rows)

    my_rows = rows_from(me_d, my_z)
    side = lax.rem(me_d + nd - 1 + 2 * my_z, nd)

    def tok_cols(r):
        return pl.ds(pl.multiple_of(r * dpart, 128), dpart)

    def cot_cols(r):
        return pl.ds(pl.multiple_of(r * fpart, 128), fpart)

    exchanged = []
    low, high = me_e - 2 * my_z, me_e - 2 * my_z + 2
    split = tok_rows // 2
    parts = ((0, split, 0, dpart), (split, split, 0, dpart), (0, tok_rows, dpart, fpart))

    def part_of(kind, first):
        row, height, col, wide = parts[kind]
        return rx.at[pl.ds(pl.multiple_of(first + row, split), height), pl.ds(col, wide)]

    def first_row(dp, z):
        return (z * nd + dp) * tok_rows

    for kind, (row, height, col, wide) in enumerate(parts):
        for way, (dp, expert, number) in enumerate(
            ((opp, pair, 2), (right, low, my_z), (left, high, my_z), (me_d, pair, 3))
        ):
            src = tokens.at[pl.ds(row, height), tok_cols(dp)] if col == 0 else cot.at[:, cot_cols(dp)]
            dst = part_of(kind, first_row(me_d, my_z))
            copy = remote(src, dst, ex_send.at[kind, way], ex_recv.at[kind, number], dp, expert)
            copy.start()
            exchanged.append(copy)
    w_swap.start()
    own_x = pltpu.make_async_copy(tokens.at[:, tok_cols(me_d)], rx.at[my_rows, pl.ds(0, dpart)], loc_sem.at[0])
    own_c = pltpu.make_async_copy(cot.at[:, cot_cols(me_d)], rx.at[my_rows, pl.ds(dpart, fpart)], loc_sem.at[1])
    own_w = pltpu.make_async_copy(w.at[0], w_own, loc_sem.at[2])
    own_x.start()
    own_c.start()
    own_w.start()

    experts_col = lax.broadcasted_iota(i32, (ne, tok_rows), 0)
    live = lax.broadcasted_iota(i32, (ne, tok_rows), 1) < count[0]
    every = jnp.zeros((ne, tok_rows), f32)
    for k in range(top):
        every = every + jnp.where((ids[pl.ds(k, 1), :] == experts_col) & live, 1.0, 0.0)
    earlier = jnp.where(
        lax.broadcasted_iota(i32, (tok_rows, tok_rows), 0) < lax.broadcasted_iota(i32, (tok_rows, tok_rows), 1), 1.0, 0.0
    )
    ranked = jnp.dot(every.astype(bf16), earlier.astype(bf16), preferred_element_type=f32)
    flag_row = jnp.broadcast_to(flags[...], (ne, ne))
    expert_row = lax.broadcasted_iota(i32, (ne, ne), 0)
    flag_col = jnp.sum(jnp.where(expert_row == lax.broadcasted_iota(i32, (ne, ne), 1), flag_row, 0), axis=1, keepdims=True)
    expert_col = lax.broadcasted_iota(i32, (ne, 1), 0)
    slot_col = jnp.where(flag_col == 1, lax.rem(expert_col + ne // 2, ne), expert_col).astype(f32) + 1.0
    for k in range(top):
        hit = (ids[pl.ds(k, 1), :] == experts_col) & live
        slot = jnp.sum(jnp.where(hit, slot_col, 0.0), axis=0, keepdims=True)
        rank = jnp.sum(jnp.where(hit, ranked, 0.0), axis=0, keepdims=True)
        aux[pl.ds(k, 1), :] = slot - 1.0
        aux[pl.ds(top + k, 1), :] = rank + ((my_z * nd + me_d) * most + 1)
    aux[pl.ds(2 * top, top), :] = gates[...]
    my_source = my_z * nd + me_d
    aux_in[my_source] = aux[...]
    for n, (i, e) in enumerate(others):
        copy = remote(aux, aux_in.at[my_source], a_send.at[n], a_recv.at[n], lax.rem(me_d + i, nd), e)
        copy.start()
        exchanged.append(copy)

    for kind in range(len(parts)):
        for number, dp, z in ((1 - my_z, side, 1 - my_z), (my_z, side, my_z), (2, opp, 1 - my_z)):
            at = part_of(kind, first_row(dp, z))
            pltpu.make_async_copy(at, at, ex_recv.at[kind, number]).wait()
            copy = remote(at, at, f_send.at[kind, number], f_recv.at[kind, number], me_d, pair)
            copy.start()
            exchanged.append(copy)
    own_x.wait()
    own_c.wait()
    for kind in range(len(parts)):
        at = part_of(kind, 0)
        pltpu.make_async_copy(at, at, ex_recv.at[kind, 3]).wait()
        for number in range(3):
            pltpu.make_async_copy(at, at, f_recv.at[kind, number]).wait()
    for n in range(len(others)):
        pltpu.make_async_copy(aux, aux, a_recv.at[n]).wait()

    lanes = sources * tok_rows
    to_slot, to_row, gate = (
        jnp.concatenate([aux_in[g, pl.ds(part * top, top), :] for g in range(sources)], axis=1) for part in range(3)
    )
    slots = expert_at(lax.broadcasted_iota(i32, (nh, lanes), 0)).astype(f32)
    place = jnp.zeros((nh, lanes), f32)
    scale = jnp.zeros((nh, lanes), f32)
    for k in range(top):
        hit = slots == to_slot[k : k + 1]
        place = jnp.where(hit, to_row[k : k + 1], place)
        scale = jnp.where(hit, gate[k : k + 1], scale)
    places[...] = place
    weights[...] = scale
    my_at = pl.ds(pl.multiple_of(here * per_slot, per_slot), per_slot)

    def rows_of(slot):
        return pl.ds(pl.multiple_of(slot * per_slot, per_slot), per_slot)

    picked = (slots_plane, per_slot, lanes)
    number = (lax.broadcasted_iota(i32, picked, 1) + 1).astype(f32)
    for d in near_first:
        plane = lax.rem(my_plane + d, planes)
        plane_slots = pl.ds(pl.multiple_of(plane * slots_plane, slots_plane), slots_plane)
        hit = jnp.broadcast_to(places[plane_slots, :][:, None, :], picked) == number
        picker = jnp.where(hit, 1.0, 0.0).astype(bf16).reshape(rows_plane, lanes)
        gated = jnp.where(hit, jnp.broadcast_to(weights[plane_slots, :][:, None, :], picked), 0.0)
        gated = gated.astype(bf16).reshape(rows_plane, lanes)
        plane_rows = pl.ds(pl.multiple_of(plane * rows_plane, rows_plane), rows_plane)
        xs = jnp.dot(picker, rx[:, pl.ds(0, dpart)], preferred_element_type=f32)
        cs = jnp.dot(gated, rx[:, pl.ds(dpart, fpart)], preferred_element_type=f32)
        send[plane_rows, pl.ds(0, dpart)] = xs.astype(bf16)
        send[plane_rows, pl.ds(dpart, fpart)] = cs.astype(bf16)

        def dispatch(step, carry, d=d, plane=plane):
            slot = plane * slots_plane + lax.rem(here + step, slots_plane)
            pltpu.make_async_remote_copy(
                src_ref=send.at[rows_of(slot)], dst_ref=got.at[my_at],
                send_sem=d_send.at[d], recv_sem=d_recv.at[d],
                device_id={"expert": expert_at(slot)}, device_id_type=MESH,
            ).start()
            return carry

        lax.fori_loop(1 if d == 0 else 0, slots_plane, dispatch, 0)
    own_rows = pltpu.make_async_copy(send.at[my_at], got.at[my_at], loc_sem.at[3])
    own_rows.start()

    own_w.wait()
    w_swap.wait()
    steps = 7
    w_rows = w_own.shape[0] // steps

    mine = lax.broadcasted_iota(i32, (1, ne), 1) == me_e
    own_flag = jnp.sum(jnp.where(mine, flags[...], 0), axis=1, keepdims=True)

    def choose(i, carry):
        at = pl.ds(pl.multiple_of(i * w_rows, w_rows), w_rows)
        w_own[at] = jnp.where(own_flag == 1, w_mov[at].astype(f32), w_own[at].astype(f32)).astype(bf16)
        return carry

    lax.fori_loop(0, steps, choose, 0)
    w_save = pltpu.make_async_copy(w_own, w_in, loc_sem.at[4])
    w_save.start()

    def ring(kind, q, src, dst, to):
        return pltpu.make_async_remote_copy(
            src_ref=src, dst_ref=dst, send_sem=r_send.at[kind, q], recv_sem=r_recv.at[kind, q],
            device_id={"dp": to}, device_id_type=MESH,
        )

    head, tail = pl.ds(0, half), pl.ds(half, half)
    at_plane = [
        pl.multiple_of(lax.rem(my_plane + planes - d, planes) * rows_plane, rows_plane) for d in near_first
    ]
    pending = []

    def go(copy):
        copy.start()
        pending.append(copy)
        return copy

    copies = {}

    def bytes_of(blocks):
        return got.at[pl.ds(0, blocks * per_slot)]

    def partials(q):
        d = near_first[q]
        blocks = slots_plane - 1 if d == 0 else slots_plane
        pltpu.make_async_copy(bytes_of(blocks), bytes_of(blocks), d_recv.at[d]).wait()
        if d == 0:
            own_rows.wait()
        x = got[pl.ds(at_plane[q], rows_plane), pl.ds(0, dpart)]

        def part(r):
            cols = pl.ds(pl.multiple_of(r * fpart, 128), fpart)
            return jnp.dot(x, w_own[:, cols], preferred_element_type=f32)

        z_send[0, q] = part(opp).astype(bf16)
        copies[0, q] = go(ring(0, q, z_send.at[0, q, head], z_first.at[0, q], right))
        copies[1, q] = go(ring(1, q, z_send.at[0, q, tail], z_first.at[1, q], left))
        z_send[1, q] = part(right).astype(bf16)
        copies[2, q] = go(ring(2, q, z_send.at[1, q, tail], z_left_in.at[q, tail], right))
        z_send[2, q] = part(left).astype(bf16)
        copies[3, q] = go(ring(3, q, z_send.at[2, q, head], z_right_in.at[q, head], left))
        z_own[q] = part(me_d)

    def pass_on(q):
        copies[0, q].wait_recv()
        z_send[1, q, head] = (z_send[1, q, head].astype(f32) + z_first[0, q].astype(f32)).astype(bf16)
        copies[4, q] = go(ring(4, q, z_send.at[1, q, head], z_left_in.at[q, head], right))
        copies[1, q].wait_recv()
        z_send[2, q, tail] = (z_send[2, q, tail].astype(f32) + z_first[1, q].astype(f32)).astype(bf16)
        copies[5, q] = go(ring(5, q, z_send.at[2, q, tail], z_right_in.at[q, tail], left))

    def finish(q):
        for kind in (2, 3, 4, 5):
            copies[kind, q].wait_recv()
        z = z_own[q] + z_left_in[q].astype(f32) + z_right_in[q].astype(f32)
        sigm = 1.0 / (1.0 + jnp.exp(-z))
        g_cot = got[pl.ds(at_plane[q], rows_plane), pl.ds(dpart, fpart)].astype(f32)
        own_slope[q] = (g_cot * sigm * (1.0 + z * (1.0 - sigm))).astype(bf16)
        at = slopes.at[me_d, pl.ds(at_plane[q], rows_plane)]
        copies[6, q] = go(ring(6, q, own_slope.at[q], at, right))
        copies[7, q] = go(ring(7, q, own_slope.at[q], at, left))
        pltpu.make_async_copy(own_slope.at[q], at, loc_sem.at[5 + q]).start()

    def forward(q):
        copies[6, q].wait_recv()
        at = slopes.at[left, pl.ds(at_plane[q], half)]
        copies[8, q] = go(ring(8, q, at, at, right))
        copies[7, q].wait_recv()
        at = slopes.at[right, pl.ds(at_plane[q] + half, half)]
        copies[9, q] = go(ring(9, q, at, at, left))

    def moments(q):
        kind, piece = divmod(q, pieces)
        source, target = ((m, m_in), (v, v_in))[kind]
        size = target.shape[0] // pieces
        at = pl.ds(piece * size, size)
        copies["swap", q] = swap(1 + kind, source.at[0, at], target.at[at])
        copies["swap", q].start()

    for step, q in order:
        (partials, pass_on, finish, forward, moments)[step](q)

    copies["x"] = pltpu.make_async_copy(got.at[:, pl.ds(0, dpart)], x_out, loc_sem.at[9])
    copies["x"].start()

    for q in range(planes):
        copies[8, q].wait_recv()
        copies[9, q].wait_recv()
        pltpu.make_async_copy(own_slope.at[q], slopes.at[me_d, pl.ds(at_plane[q], rows_plane)], loc_sem.at[5 + q]).wait()
    for copy in pending + exchanged:
        copy.wait_send()
    for d in near_first:
        blocks = slots_plane - 1 if d == 0 else slots_plane
        pltpu.make_async_copy(bytes_of(blocks), bytes_of(blocks), d_send.at[d]).wait()
    copies["x"].wait()
    w_save.wait()
    for kind, target in ((1, m_in), (2, v_in)):
        pltpu.make_async_copy(target, target, swap_recv.at[kind]).wait()
        pltpu.make_async_copy(target, target, swap_send.at[kind]).wait()


def exchange(nd, ne, count, ids, gates, flags, tokens, cot, w, m, v):
    tok_rows, width = tokens.shape
    hidden = cot.shape[1]
    dpart, fpart = width // nd, hidden // nd
    planes = 4
    rows = ne * nd * most
    rows_plane = rows // planes
    half = rows_plane // 2
    top = ids.shape[0]
    vm = pl.BlockSpec(memory_space=pltpu.VMEM)
    hbm = pl.BlockSpec(memory_space=pl.ANY)
    state = jax.ShapeDtypeStruct((dpart, hidden), bf16)
    dma = pltpu.SemaphoreType.DMA
    return pl.pallas_call(
        functools.partial(exchange_kernel, nd, ne, planes),
        out_shape=(
            jax.ShapeDtypeStruct((rows, dpart), bf16),
            jax.ShapeDtypeStruct((nd, rows, fpart), bf16),
            state, state, state,
        ),
        in_specs=[pl.BlockSpec(memory_space=pltpu.SMEM)] + [vm] * 3 + [hbm] * 5,
        out_specs=(hbm,) * 5,
        scratch_shapes=[
            pltpu.VMEM((2 * nd * tok_rows, dpart + fpart), bf16),
            pltpu.VMEM((3 * top, tok_rows), f32),
            pltpu.VMEM((2 * nd, 3 * top, tok_rows), f32),
            pltpu.VMEM((ne // 2, 2 * nd * tok_rows), f32),
            pltpu.VMEM((ne // 2, 2 * nd * tok_rows), f32),
            pltpu.VMEM((rows, dpart + fpart), bf16),
            pltpu.VMEM((rows, dpart + fpart), bf16),
            pltpu.VMEM((dpart, hidden), bf16),
            pltpu.VMEM((dpart, hidden), bf16),
            pltpu.VMEM((3, planes, rows_plane, fpart), bf16),
            pltpu.VMEM((planes, rows_plane, fpart), f32),
            pltpu.VMEM((2, planes, half, fpart), bf16),
            pltpu.VMEM((planes, rows_plane, fpart), bf16),
            pltpu.VMEM((planes, rows_plane, fpart), bf16),
            pltpu.VMEM((planes, rows_plane, fpart), bf16),
            dma((10,)), dma((3,)), dma((3,)), dma((3, 4)), dma((3, 4)),
            dma((2 * nd - 1,)), dma((2 * nd - 1,)), dma((3, 3)), dma((3, 3)),
            dma((planes,)), dma((planes,)), dma((10, planes)), dma((10, planes)),
        ],
        compiler_params=pltpu.CompilerParams(collective_id=0, has_side_effects=True, vmem_limit_bytes=56 << 20),
    )(count, ids, gates, flags, tokens, cot, w, m, v)


def update_kernel(flags, me, x, slopes, w, m, v, m_in, v_in, w_new, m_new, v_new):
    swapped = flags[me[0]] == 1
    nd, _, fpart = slopes.shape
    for r in range(nd):
        cols = pl.ds(r * fpart, fpart)
        grad = lax.dot_general(x[...], slopes[r], (((0,), (0,)), ((), ())), preferred_element_type=f32)
        first = jnp.where(swapped, m_in[:, cols].astype(f32), m[0, :, cols].astype(f32))
        second = jnp.where(swapped, v_in[:, cols].astype(f32), v[0, :, cols].astype(f32))
        first_new = beta_first * first + (1.0 - beta_first) * grad
        second_new = beta_second * second + (1.0 - beta_second) * grad * grad
        ratio = first_new * (1.0 / bias_first) / (jnp.sqrt(second_new * (1.0 / bias_second)) + epsilon)
        w_new[0, :, cols] = (w[:, cols].astype(f32) - learn_rate * ratio).astype(bf16)
        m_new[0, :, cols] = first_new.astype(bf16)
        v_new[0, :, cols] = second_new.astype(bf16)


def update(flags, me, x, slopes, w, m, v, m_in, v_in):
    rows, dpart = x.shape
    nd, _, fpart = slopes.shape
    hidden = nd * fpart
    block = 128
    state = jax.ShapeDtypeStruct((1, dpart, hidden), bf16)
    here = pl.BlockSpec((1, block, hidden), lambda i, flags, me: (0, i, 0))
    stays = pl.BlockSpec((1, block, hidden), lambda i, flags, me: (0, i * (1 - flags[me[0]]), 0))
    moved = pl.BlockSpec((block, hidden), lambda i, flags, me: (i * flags[me[0]], 0))
    return pl.pallas_call(
        update_kernel,
        out_shape=(state, state, state),
        grid_spec=pltpu.PrefetchScalarGridSpec(
            num_scalar_prefetch=2,
            grid=(dpart // block,),
            in_specs=[
                pl.BlockSpec((rows, block), lambda i, flags, me: (0, i)),
                pl.BlockSpec((nd, rows, fpart), lambda i, flags, me: (0, 0, 0)),
                pl.BlockSpec((block, hidden), lambda i, flags, me: (i, 0)),
                stays, stays, moved, moved,
            ],
            out_specs=(here, here, here),
        ),
        compiler_params=pltpu.CompilerParams(vmem_limit_bytes=60 << 20),
    )(flags, me, x, slopes, w, m, v, m_in, v_in)


def shards(tokens, cotangent, expert_ids, gate_values, counts, swap_flags, weights, first_moment, second_moment):
    ne, nd = lax.axis_size("expert"), lax.axis_size("dp")
    x, slopes, w_in, m_in, v_in = exchange(
        nd, ne, counts, expert_ids.T, gate_values.T, swap_flags[None], tokens, cotangent, weights, first_moment, second_moment
    )
    me = lax.axis_index("expert").astype(i32)[None]
    return update(swap_flags, me, x, slopes, w_in, first_moment, second_moment, m_in, v_in)


def solution(mesh):
    placed = (
        P(("dp", "expert"), None),
        P(("dp", "expert"), None),
        P(("dp", "expert"), None),
        P(("dp", "expert"), None),
        P(("dp", "expert")),
        P(),
        P("expert", "dp", None),
        P("expert", "dp", None),
        P("expert", "dp", None),
    )
    return jax.shard_map(
        shards,
        mesh=mesh,
        in_specs=placed,
        out_specs=(P("expert", "dp", None), P("expert", "dp", None), P("expert", "dp", None)),
        check_vma=False,
    )
```

profile of v0, /device:TPU:5, one launch (start us, length us, event | category | flops | bytes accessed | tf_op | source)
XLA Modules:
  0.0 201.8 jit_solution(15990398300500962201)
XLA Ops:
  1.3 187.6 %shard_map.112 = (bf16[1536,896]{1,0:T(8,128)(2,1)}, bf16[4,1536,256]{2,1,0:T(8,128)(2,1)}, bf16[896,1024]{1,0:T(8,128)(2,1)}, bf16[896,1024]{1,0:T(8,128)(2,1)}, bf16[896,1024]{1,0:T(8,128)(2,1)}) custom-call(s32[1]{0:T(128)S(6)} %copy.12.count, s32[8,128]{1,0:T(8,128)} %bitcast.4, f32[8,128]{1,0:T(8,128)} %bitcast.5, s32[1,64]{1,0:T(1,128)} %bitcast.6, ...), custom_call_target="tpu_custom_call" | custom-call | tf_op jit(solution)/shard_map/pallas_call | solution.py:344
  188.9 12.9 %shard_map.113 = (bf16[1,896,1024]{2,1,0:T(8,128)(2,1)}, bf16[1,896,1024]{2,1,0:T(8,128)(2,1)}, bf16[1,896,1024]{2,1,0:T(8,128)(2,1)}) custom-call(s32[64]{0:T(128)} %flags.1, s32[1]{0:T(128)} %bitcast.me, bf16[1536,896]{1,0:T(8,128)(2,1)} %get-tuple-element.8.x, bf16[4,1536,256]{2,1,0:T(8,128)(2,1)} %get-tuple-element.9.slopes, ...), custom_call_target="tpu_custom_call" | custom-call | tf_op jit(solution)/shard_map/pallas_call | solution.py:402
where the time goes:
time: 202 us
  Pallas kernels  201 us (100%)
    pallas_call x1, Pallas kernels, exchange(): pl.pallas_call(functools.partial(exchange_kernel, nd, ne, planes), out_sh...  188 us
    pallas_call x1, Pallas kernels, update(): pl.pallas_call(update_kernel, out_shape=(state, state, state), grid_spec=...  12.9 us

commit v1 on v0

--- a/solution.py
+++ b/solution.py
@@ -17,18 +17,18 @@
 f32, bf16, i32 = jnp.float32, jnp.bfloat16, jnp.int32
 MESH = pl.DeviceIdType.MESH
 near_first = (0, 1, 3, 2)
-pieces = 1
-PART, PASS, FINISH, FORWARD, MOMENTS = range(5)
+pieces = ((0, 0, 256), (0, 256, 640), (1, 0, 896))
+PART, PASS, FINISH, FORWARD, MOMENTS, GRAD, PICK = range(7)
 order = (
-    (PART, 0), (PASS, 0), (PART, 1), (PASS, 1), (PART, 2), (MOMENTS, 0), (MOMENTS, 1), (FINISH, 0), (PASS, 2), (FINISH, 1), (FORWARD, 0), (PART, 3), (FORWARD, 1), (FINISH, 2), (PASS, 3), (FORWARD, 2), (FINISH, 3), (FORWARD, 3),
+    (PICK, 0), (PICK, 1), (PICK, 2), (PART, 0), (PICK, 3), (PASS, 0), (PART, 1), (PASS, 1), (PART, 2), (MOMENTS, 1), (MOMENTS, 2), (FINISH, 0), (PASS, 2), (FINISH, 1), (FORWARD, 0), (PART, 3), (FORWARD, 1), (FINISH, 2), (PASS, 3), (GRAD, 0), (FORWARD, 2), (FINISH, 3), (GRAD, 1), (FORWARD, 3), (GRAD, 2),
 )
 
 
 def exchange_kernel(
     nd, ne, planes,
     count, ids, gates, flags, tokens, cot, w, m, v,
-    x_out, slopes, w_in, m_in, v_in,
-    rx, aux, aux_in, places, weights, send, got, w_own, w_mov, z_send, z_own, z_first, z_right_in, z_left_in, own_slope,
+    x_last, s_last, g_out, w_in, m_in, v_in,
+    rx, aux, aux_in, places, weights, send, got, w_own, w_mov, z_send, z_own, z_first, z_right_in, z_left_in, slopes, g_sum,
     loc_sem, swap_send, swap_recv, ex_send, ex_recv, a_send, a_recv, f_send, f_recv, d_send, d_recv, r_send, r_recv,
 ):
     me_d, me_e = lax.axis_index("dp"), lax.axis_index("expert")
@@ -111,7 +111,14 @@
             copy = remote(src, dst, ex_send.at[kind, way], ex_recv.at[kind, number], dp, expert)
             copy.start()
             exchanged.append(copy)
+    def moments(q):
+        kind, first, height = pieces[q]
+        source, target = ((m, m_in), (v, v_in))[kind]
+        at = pl.ds(first, height)
+        swap(1 + kind, source.at[0, at], target.at[at]).start()
+
     w_swap.start()
+    moments(0)
     own_x = pltpu.make_async_copy(tokens.at[:, tok_cols(me_d)], rx.at[my_rows, pl.ds(0, dpart)], loc_sem.at[0])
     own_c = pltpu.make_async_copy(cot.at[:, cot_cols(me_d)], rx.at[my_rows, pl.ds(dpart, fpart)], loc_sem.at[1])
     own_w = pltpu.make_async_copy(w.at[0], w_own, loc_sem.at[2])
@@ -154,6 +161,23 @@
             copy = remote(at, at, f_send.at[kind, number], f_recv.at[kind, number], me_d, pair)
             copy.start()
             exchanged.append(copy)
+    own_w.wait()
+    w_swap.wait()
+    steps = 7
+    w_rows = w_own.shape[0] // steps
+
+    mine = lax.broadcasted_iota(i32, (1, ne), 1) == me_e
+    own_flag = jnp.sum(jnp.where(mine, flags[...], 0), axis=1, keepdims=True)
+
+    def choose(i, carry):
+        at = pl.ds(pl.multiple_of(i * w_rows, w_rows), w_rows)
+        w_own[at] = jnp.where(own_flag == 1, w_mov[at].astype(f32), w_own[at].astype(f32)).astype(bf16)
+        return carry
+
+    lax.fori_loop(0, steps, choose, 0)
+    w_save = pltpu.make_async_copy(w_own, w_in, loc_sem.at[4])
+    w_save.start()
+
     own_x.wait()
     own_c.wait()
     for kind in range(len(parts)):
@@ -184,7 +208,10 @@
 
     picked = (slots_plane, per_slot, lanes)
     number = (lax.broadcasted_iota(i32, picked, 1) + 1).astype(f32)
-    for d in near_first:
+    own_rows = pltpu.make_async_copy(send.at[my_at], got.at[my_at], loc_sem.at[3])
+
+    def pick(q):
+        d = near_first[q]
         plane = lax.rem(my_plane + d, planes)
         plane_slots = pl.ds(pl.multiple_of(plane * slots_plane, slots_plane), slots_plane)
         hit = jnp.broadcast_to(places[plane_slots, :][:, None, :], picked) == number
@@ -197,7 +224,7 @@
         send[plane_rows, pl.ds(0, dpart)] = xs.astype(bf16)
         send[plane_rows, pl.ds(dpart, fpart)] = cs.astype(bf16)
 
-        def dispatch(step, carry, d=d, plane=plane):
+        def dispatch(step, carry):
             slot = plane * slots_plane + lax.rem(here + step, slots_plane)
             pltpu.make_async_remote_copy(
                 src_ref=send.at[rows_of(slot)], dst_ref=got.at[my_at],
@@ -207,25 +234,8 @@
             return carry
 
         lax.fori_loop(1 if d == 0 else 0, slots_plane, dispatch, 0)
-    own_rows = pltpu.make_async_copy(send.at[my_at], got.at[my_at], loc_sem.at[3])
-    own_rows.start()
-
-    own_w.wait()
-    w_swap.wait()
-    steps = 7
-    w_rows = w_own.shape[0] // steps
-
-    mine = lax.broadcasted_iota(i32, (1, ne), 1) == me_e
-    own_flag = jnp.sum(jnp.where(mine, flags[...], 0), axis=1, keepdims=True)
-
-    def choose(i, carry):
-        at = pl.ds(pl.multiple_of(i * w_rows, w_rows), w_rows)
-        w_own[at] = jnp.where(own_flag == 1, w_mov[at].astype(f32), w_own[at].astype(f32)).astype(bf16)
-        return carry
-
-    lax.fori_loop(0, steps, choose, 0)
-    w_save = pltpu.make_async_copy(w_own, w_in, loc_sem.at[4])
-    w_save.start()
+        if d == 0:
+            own_rows.start()
 
     def ring(kind, q, src, dst, to):
         return pltpu.make_async_remote_copy(
@@ -237,7 +247,7 @@
     at_plane = [
         pl.multiple_of(lax.rem(my_plane + planes - d, planes) * rows_plane, rows_plane) for d in near_first
     ]
-    pending = []
+    pending, settled = [], []
 
     def go(copy):
         copy.start()
@@ -255,6 +265,10 @@
         pltpu.make_async_copy(bytes_of(blocks), bytes_of(blocks), d_recv.at[d]).wait()
         if d == 0:
             own_rows.wait()
+        if q == planes - 1:
+            rows_out = got.at[pl.ds(at_plane[q], rows_plane), pl.ds(0, dpart)]
+            copies["x"] = pltpu.make_async_copy(rows_out, x_last, loc_sem.at[6])
+            copies["x"].start()
         x = got[pl.ds(at_plane[q], rows_plane), pl.ds(0, dpart)]
 
         def part(r):
@@ -284,44 +298,63 @@
         z = z_own[q] + z_left_in[q].astype(f32) + z_right_in[q].astype(f32)
         sigm = 1.0 / (1.0 + jnp.exp(-z))
         g_cot = got[pl.ds(at_plane[q], rows_plane), pl.ds(dpart, fpart)].astype(f32)
-        own_slope[q] = (g_cot * sigm * (1.0 + z * (1.0 - sigm))).astype(bf16)
-        at = slopes.at[me_d, pl.ds(at_plane[q], rows_plane)]
-        copies[6, q] = go(ring(6, q, own_slope.at[q], at, right))
-        copies[7, q] = go(ring(7, q, own_slope.at[q], at, left))
-        pltpu.make_async_copy(own_slope.at[q], at, loc_sem.at[5 + q]).start()
+        slope = (g_cot * sigm * (1.0 + z * (1.0 - sigm))).astype(bf16)
+        if q < planes - 1:
+            slopes[q, me_d] = slope
+            src = slopes.at[q, me_d]
+        else:
+            for kind in (0, 1):
+                copies[kind, q].wait_send()
+                settled.append(copies[kind, q])
+            z_send[0, q] = slope
+            src = z_send.at[0, q]
+            copies["s"] = pltpu.make_async_copy(src, s_last.at[me_d], loc_sem.at[5])
+            copies["s"].start()
+        at = block_of(q, me_d, 0, rows_plane)
+        copies[6, q] = go(ring(6, q, src, at, right))
+        copies[7, q] = go(ring(7, q, src, at, left))
+
+    def block_of(q, dp, first, height):
+        held = slopes.at[q] if q < planes - 1 else s_last
+        return held.at[dp, pl.ds(first, height)]
 
     def forward(q):
         copies[6, q].wait_recv()
-        at = slopes.at[left, pl.ds(at_plane[q], half)]
+        at = block_of(q, left, 0, half)
         copies[8, q] = go(ring(8, q, at, at, right))
         copies[7, q].wait_recv()
-        at = slopes.at[right, pl.ds(at_plane[q] + half, half)]
+        at = block_of(q, right, half, half)
         copies[9, q] = go(ring(9, q, at, at, left))
 
-    def moments(q):
-        kind, piece = divmod(q, pieces)
-        source, target = ((m, m_in), (v, v_in))[kind]
-        size = target.shape[0] // pieces
-        at = pl.ds(piece * size, size)
-        copies["swap", q] = swap(1 + kind, source.at[0, at], target.at[at])
-        copies["swap", q].start()
-
-    for step, q in order:
-        (partials, pass_on, finish, forward, moments)[step](q)
-
-    copies["x"] = pltpu.make_async_copy(got.at[:, pl.ds(0, dpart)], x_out, loc_sem.at[9])
-    copies["x"].start()
-
-    for q in range(planes):
+    def gradient(q):
         copies[8, q].wait_recv()
         copies[9, q].wait_recv()
-        pltpu.make_async_copy(own_slope.at[q], slopes.at[me_d, pl.ds(at_plane[q], rows_plane)], loc_sem.at[5 + q]).wait()
+        x = got[pl.ds(at_plane[q], rows_plane), pl.ds(0, dpart)]
+        for r in range(nd):
+            cols = pl.ds(r * fpart, fpart)
+            more = lax.dot_general(x, slopes[q, r], (((0,), (0,)), ((), ())), preferred_element_type=f32)
+            if q == 0:
+                g_sum[:, cols] = more
+            else:
+                g_sum[:, cols] = g_sum[:, cols] + more
+
+    for step, q in order:
+        (partials, pass_on, finish, forward, moments, gradient, pick)[step](q)
+
+    g_save = pltpu.make_async_copy(g_sum, g_out, loc_sem.at[7])
+    g_save.start()
+
+    copies[8, planes - 1].wait_recv()
+    copies[9, planes - 1].wait_recv()
     for copy in pending + exchanged:
-        copy.wait_send()
+        if not any(copy is other for other in settled):
+            copy.wait_send()
     for d in near_first:
         blocks = slots_plane - 1 if d == 0 else slots_plane
         pltpu.make_async_copy(bytes_of(blocks), bytes_of(blocks), d_send.at[d]).wait()
     copies["x"].wait()
+    copies["s"].wait()
+    g_save.wait()
     w_save.wait()
     for kind, target in ((1, m_in), (2, v_in)):
         pltpu.make_async_copy(target, target, swap_recv.at[kind]).wait()
@@ -344,12 +377,13 @@
     return pl.pallas_call(
         functools.partial(exchange_kernel, nd, ne, planes),
         out_shape=(
-            jax.ShapeDtypeStruct((rows, dpart), bf16),
-            jax.ShapeDtypeStruct((nd, rows, fpart), bf16),
+            jax.ShapeDtypeStruct((rows_plane, dpart), bf16),
+            jax.ShapeDtypeStruct((nd, rows_plane, fpart), bf16),
+            jax.ShapeDtypeStruct((dpart, hidden), f32),
             state, state, state,
         ),
         in_specs=[pl.BlockSpec(memory_space=pltpu.SMEM)] + [vm] * 3 + [hbm] * 5,
-        out_specs=(hbm,) * 5,
+        out_specs=(hbm,) * 6,
         scratch_shapes=[
             pltpu.VMEM((2 * nd * tok_rows, dpart + fpart), bf16),
             pltpu.VMEM((3 * top, tok_rows), f32),
@@ -365,7 +399,8 @@
             pltpu.VMEM((2, planes, half, fpart), bf16),
             pltpu.VMEM((planes, rows_plane, fpart), bf16),
             pltpu.VMEM((planes, rows_plane, fpart), bf16),
-            pltpu.VMEM((planes, rows_plane, fpart), bf16),
+            pltpu.VMEM((planes - 1, nd, rows_plane, fpart), bf16),
+            pltpu.VMEM((dpart, hidden), f32),
             dma((10,)), dma((3,)), dma((3,)), dma((3, 4)), dma((3, 4)),
             dma((2 * nd - 1,)), dma((2 * nd - 1,)), dma((3, 3)), dma((3, 3)),
             dma((planes,)), dma((planes,)), dma((10, planes)), dma((10, planes)),
@@ -374,23 +409,33 @@
     )(count, ids, gates, flags, tokens, cot, w, m, v)
 
 
-def update_kernel(flags, me, x, slopes, w, m, v, m_in, v_in, w_new, m_new, v_new):
+def update_kernel(flags, me, x, slopes, g, w, m, v, m_in, v_in, w_new, m_new, v_new):
     swapped = flags[me[0]] == 1
     nd, _, fpart = slopes.shape
-    for r in range(nd):
-        cols = pl.ds(r * fpart, fpart)
-        grad = lax.dot_general(x[...], slopes[r], (((0,), (0,)), ((), ())), preferred_element_type=f32)
-        first = jnp.where(swapped, m_in[:, cols].astype(f32), m[0, :, cols].astype(f32))
-        second = jnp.where(swapped, v_in[:, cols].astype(f32), v[0, :, cols].astype(f32))
-        first_new = beta_first * first + (1.0 - beta_first) * grad
-        second_new = beta_second * second + (1.0 - beta_second) * grad * grad
-        ratio = first_new * (1.0 / bias_first) / (jnp.sqrt(second_new * (1.0 / bias_second)) + epsilon)
-        w_new[0, :, cols] = (w[:, cols].astype(f32) - learn_rate * ratio).astype(bf16)
-        m_new[0, :, cols] = first_new.astype(bf16)
-        v_new[0, :, cols] = second_new.astype(bf16)
-
-
-def update(flags, me, x, slopes, w, m, v, m_in, v_in):
+
+    def step(first_of, second_of):
+        for r in range(nd):
+            cols = pl.ds(r * fpart, fpart)
+            last = lax.dot_general(x[...], slopes[r], (((0,), (0,)), ((), ())), preferred_element_type=f32)
+            grad = g[:, cols] + last
+            first_new = beta_first * first_of(cols).astype(f32) + (1.0 - beta_first) * grad
+            second_new = beta_second * second_of(cols).astype(f32) + (1.0 - beta_second) * grad * grad
+            scaled = second_new * (1.0 / bias_second)
+            ratio = first_new * (learn_rate / bias_first) / (scaled * lax.rsqrt(scaled) + epsilon)
+            w_new[0, :, cols] = (w[:, cols].astype(f32) - ratio).astype(bf16)
+            m_new[0, :, cols] = first_new.astype(bf16)
+            v_new[0, :, cols] = second_new.astype(bf16)
+
+    @pl.when(swapped)
+    def _():
+        step(lambda cols: m_in[:, cols], lambda cols: v_in[:, cols])
+
+    @pl.when(jnp.logical_not(swapped))
+    def _():
+        step(lambda cols: m[0, :, cols], lambda cols: v[0, :, cols])
+
+
+def update(flags, me, x, slopes, g, w, m, v, m_in, v_in):
     rows, dpart = x.shape
     nd, _, fpart = slopes.shape
     hidden = nd * fpart
@@ -409,21 +454,22 @@
                 pl.BlockSpec((rows, block), lambda i, flags, me: (0, i)),
                 pl.BlockSpec((nd, rows, fpart), lambda i, flags, me: (0, 0, 0)),
                 pl.BlockSpec((block, hidden), lambda i, flags, me: (i, 0)),
+                pl.BlockSpec((block, hidden), lambda i, flags, me: (i, 0)),
                 stays, stays, moved, moved,
             ],
             out_specs=(here, here, here),
         ),
         compiler_params=pltpu.CompilerParams(vmem_limit_bytes=60 << 20),
-    )(flags, me, x, slopes, w, m, v, m_in, v_in)
+    )(flags, me, x, slopes, g, w, m, v, m_in, v_in)
 
 
 def shards(tokens, cotangent, expert_ids, gate_values, counts, swap_flags, weights, first_moment, second_moment):
     ne, nd = lax.axis_size("expert"), lax.axis_size("dp")
-    x, slopes, w_in, m_in, v_in = exchange(
+    x, slopes, g, w_in, m_in, v_in = exchange(
         nd, ne, counts, expert_ids.T, gate_values.T, swap_flags[None], tokens, cotangent, weights, first_moment, second_moment
     )
     me = lax.axis_index("expert").astype(i32)[None]
-    return update(swap_flags, me, x, slopes, w_in, first_moment, second_moment, m_in, v_in)
+    return update(swap_flags, me, x, slopes, g, w_in, first_moment, second_moment, m_in, v_in)
 
 
 def solution(mesh):

time: 202 us -> 196 us (0.970)
  Pallas kernels: 201 us -> 193 us
    pallas_call x1, Pallas kernels: 188 us -> 183 us  [exchange(): pl.pallas_call(functools.partial(exchange_kernel, nd, ne, planes), out_sh...]
    pallas_call x1, Pallas kernels: 12.9 us -> 10.8 us  [update(): pl.pallas_call(update_kernel, out_shape=(state, state, state), grid_spec=...]
where the time goes in v1:
time: 196 us; the launch traced here: 195 us
  Pallas kernels  193 us (98%)
    pallas_call x1, Pallas kernels, exchange(): pl.pallas_call(functools.partial(exchange_kernel, nd, ne, planes), out_sh...  183 us
    pallas_call x1, Pallas kernels, update(): pl.pallas_call(update_kernel, out_shape=(state, state, state), grid_spec=...  10.8 us

profile of v1, /device:TPU:5, one launch (start us, length us, event | category | flops | bytes accessed | tf_op | source)
XLA Modules:
  0.0 194.8 jit_solution(14367383383493669481)
XLA Ops:
  1.3 182.6 %shard_map.112 = (bf16[384,896]{1,0:T(8,128)(2,1)}, bf16[4,384,256]{2,1,0:T(8,128)(2,1)}, f32[896,1024]{1,0:T(8,128)}, bf16[896,1024]{1,0:T(8,128)(2,1)}, bf16[8...) custom-call(s32[1]{0:T(128)S(6)} %copy.12.count, s32[8,128]{1,0:T(8,128)} %bitcast.4, f32[8,128]{1,0:T(8,128)} %bitcast.5, ...), custom_call_target="tpu_custom_call" | custom-call | tf_op jit(solution)/shard_map/pallas_call | solution.py:377
  183.9 10.8 %shard_map.113 = (bf16[1,896,1024]{2,1,0:T(8,128)(2,1)}, bf16[1,896,1024]{2,1,0:T(8,128)(2,1)}, bf16[1,896,1024]{2,1,0:T(8,128)(2,1)}) custom-call(s32[64]{0:T(128)} %flags.1, s32[1]{0:T(128)} %bitcast.me, bf16[384,896]{1,0:T(8,128)(2,1)} %get-tuple-element.9.x, bf16[4,384,256]{2,1,0:T(8,128)(2,1)} %get-tuple-element.10.slopes, ...), custom_call_target="tpu_custom_call" | custom-call | tf_op jit(solution)/shard_map/pallas_call | solution.py:447

commit v2 on v1

--- a/solution.py
+++ b/solution.py
@@ -20,7 +20,7 @@
 pieces = ((0, 0, 256), (0, 256, 640), (1, 0, 896))
 PART, PASS, FINISH, FORWARD, MOMENTS, GRAD, PICK = range(7)
 order = (
-    (PICK, 0), (PICK, 1), (PICK, 2), (PART, 0), (PICK, 3), (PASS, 0), (PART, 1), (PASS, 1), (PART, 2), (MOMENTS, 1), (MOMENTS, 2), (FINISH, 0), (PASS, 2), (FINISH, 1), (FORWARD, 0), (PART, 3), (FORWARD, 1), (FINISH, 2), (PASS, 3), (GRAD, 0), (FORWARD, 2), (FINISH, 3), (GRAD, 1), (FORWARD, 3), (GRAD, 2),
+    (PICK, 0), (PICK, 1), (PICK, 2), (PART, 0), (PICK, 3), (PASS, 0), (FINISH, 0), (PART, 1), (PASS, 1), (PART, 2), (MOMENTS, 1), (MOMENTS, 2), (FORWARD, 0), (PASS, 2), (FINISH, 1), (PART, 3), (PASS, 3), (FORWARD, 1), (FINISH, 2), (GRAD, 0), (FORWARD, 2), (FINISH, 3), (GRAD, 1), (FORWARD, 3), (GRAD, 2),
 )
 
 

time: 196 us -> 192 us (0.980)
  Pallas kernels: 193 us -> 188 us
    pallas_call x1, Pallas kernels: 183 us -> 177 us  [exchange(): pl.pallas_call(functools.partial(exchange_kernel, nd, ne, planes), out_sh...]
where the time goes in v2:
time: 192 us; the launch traced here: 190 us
  Pallas kernels  188 us (98%)
    pallas_call x1, Pallas kernels, exchange(): pl.pallas_call(functools.partial(exchange_kernel, nd, ne, planes), out_sh...  177 us
    pallas_call x1, Pallas kernels, update(): pl.pallas_call(update_kernel, out_shape=(state, state, state), grid_spec=...  10.8 us

profile of v2, /device:TPU:5, one launch (start us, length us, event | category | flops | bytes accessed | tf_op | source)
XLA Modules:
  0.0 189.7 jit_solution(1839614421428579920)
XLA Ops:
  1.3 177.5 %shard_map.112 = (bf16[384,896]{1,0:T(8,128)(2,1)}, bf16[4,384,256]{2,1,0:T(8,128)(2,1)}, f32[896,1024]{1,0:T(8,128)}, bf16[896,1024]{1,0:T(8,128)(2,1)}, bf16[8...) custom-call(s32[1]{0:T(128)S(6)} %copy.12.count, s32[8,128]{1,0:T(8,128)} %bitcast.4, f32[8,128]{1,0:T(8,128)} %bitcast.5, ...), custom_call_target="tpu_custom_call" | custom-call | tf_op jit(solution)/shard_map/pallas_call | solution.py:377
  178.8 10.8 %shard_map.113 = (bf16[1,896,1024]{2,1,0:T(8,128)(2,1)}, bf16[1,896,1024]{2,1,0:T(8,128)(2,1)}, bf16[1,896,1024]{2,1,0:T(8,128)(2,1)}) custom-call(s32[64]{0:T(128)} %flags.1, s32[1]{0:T(128)} %bitcast.me, bf16[384,896]{1,0:T(8,128)(2,1)} %get-tuple-element.9.x, bf16[4,384,256]{2,1,0:T(8,128)(2,1)} %get-tuple-element.10.slopes, ...), custom_call_target="tpu_custom_call" | custom-call | tf_op jit(solution)/shard_map/pallas_call | solution.py:447

commit v3 on v2

--- a/solution.py
+++ b/solution.py
@@ -20,7 +20,7 @@
 pieces = ((0, 0, 256), (0, 256, 640), (1, 0, 896))
 PART, PASS, FINISH, FORWARD, MOMENTS, GRAD, PICK = range(7)
 order = (
-    (PICK, 0), (PICK, 1), (PICK, 2), (PART, 0), (PICK, 3), (PASS, 0), (FINISH, 0), (PART, 1), (PASS, 1), (PART, 2), (MOMENTS, 1), (MOMENTS, 2), (FORWARD, 0), (PASS, 2), (FINISH, 1), (PART, 3), (PASS, 3), (FORWARD, 1), (FINISH, 2), (GRAD, 0), (FORWARD, 2), (FINISH, 3), (GRAD, 1), (FORWARD, 3), (GRAD, 2),
+    (PICK, 0), (PICK, 1), (PICK, 2), (PART, 0), (PICK, 3), (PASS, 0), (FINISH, 0), (PART, 1), (PASS, 1), (FORWARD, 0), (PART, 2), (MOMENTS, 1), (MOMENTS, 2), (FINISH, 1), (PASS, 2), (PART, 3), (PASS, 3), (FORWARD, 1), (FINISH, 2), (GRAD, 0), (FORWARD, 2), (FINISH, 3), (GRAD, 1), (FORWARD, 3), (GRAD, 2),
 )
 
 

time: 192 us -> 192 us (level)
  no operation moved by 1% of the time
where the time goes in v3:
time: 192 us; the launch traced here: 190 us
  Pallas kernels  188 us (98%)
    pallas_call x1, Pallas kernels, exchange(): pl.pallas_call(functools.partial(exchange_kernel, nd, ne, planes), out_sh...  178 us
    pallas_call x1, Pallas kernels, update(): pl.pallas_call(update_kernel, out_shape=(state, state, state), grid_spec=...  10.8 us

profile of v3, /device:TPU:5, one launch (start us, length us, event | category | flops | bytes accessed | tf_op | source)
XLA Modules:
  0.0 189.7 jit_solution(10345115300446386139)
XLA Ops:
  1.3 177.5 %shard_map.112 = (bf16[384,896]{1,0:T(8,128)(2,1)}, bf16[4,384,256]{2,1,0:T(8,128)(2,1)}, f32[896,1024]{1,0:T(8,128)}, bf16[896,1024]{1,0:T(8,128)(2,1)}, bf16[8...) custom-call(s32[1]{0:T(128)S(6)} %copy.12.count, s32[8,128]{1,0:T(8,128)} %bitcast.4, f32[8,128]{1,0:T(8,128)} %bitcast.5, ...), custom_call_target="tpu_custom_call" | custom-call | tf_op jit(solution)/shard_map/pallas_call | solution.py:377
  178.8 10.8 %shard_map.113 = (bf16[1,896,1024]{2,1,0:T(8,128)(2,1)}, bf16[1,896,1024]{2,1,0:T(8,128)(2,1)}, bf16[1,896,1024]{2,1,0:T(8,128)(2,1)}) custom-call(s32[64]{0:T(128)} %flags.1, s32[1]{0:T(128)} %bitcast.me, bf16[384,896]{1,0:T(8,128)(2,1)} %get-tuple-element.9.x, bf16[4,384,256]{2,1,0:T(8,128)(2,1)} %get-tuple-element.10.slopes, ...), custom_call_target="tpu_custom_call" | custom-call | tf_op jit(solution)/shard_map/pallas_call | solution.py:447
